TPU v7x, 32 devices: a whole 2x2x4 slice. The times are simulated.
32 devices in a mesh: head: 4 (over y, x), ctx: 8 (over z, core).
Axes of the slice: x: 2, y: 2, z: 4, core: 2. Of those that a mesh axis runs over, the one named last changes fastest.
Arguments:
- query_in: bfloat16 [4096, 4096], P(('ctx', 'head')), may hold values from -6 to 6
- key_in: bfloat16 [4096, 1024], P(('ctx', 'head')), may hold values from -6 to 6
- value_in: bfloat16 [4096, 1024], P(('ctx', 'head')), may hold values from -6 to 6
- attn_out: bfloat16 [4096, 4096], P(('ctx', 'head')), may hold values from -2 to 2
- out_grad: bfloat16 [4096, 4096], P(('ctx', 'head')), may hold values from -6 to 6
- log_norm: float32 [4096, 32], P(('ctx', 'head')), may hold values from 4 to 8
- doc_ids: int32 [4096], replicated, may hold values from 0 to 15, never falling along the last dimension, each value on 1 to 512 neighbouring positions
Outputs:
- query_grad: bfloat16 [4096, 4096], P(('ctx', 'head'))
- key_grad: bfloat16 [4096, 1024], P(('ctx', 'head'))
- value_grad: bfloat16 [4096, 1024], P(('ctx', 'head'))
Inputs may be any that keep to these rules, and one draw needn't show every extreme that they name: `doc_ids`: document numbers never fall along the sequence and start at 0; every document has 1 to 512 tokens and one has exactly 512.
All inputs are finite; a program needn't handle non-finite values.
Results may differ from a plain program's by a relative error of at most 0.0049.
Values may be sent and summed in bfloat16 or wider, within the bound.
No kernel may reach another device: no remote copies, remote signals or barrier semaphores. Data moves between devices by JAX's collectives and lax.ppermute only.
A program may use at most 128 MiB of HBM per device.

v0:
```python
import jax
import jax.numpy as jnp
from jax import lax
from jax.sharding import PartitionSpec as P

HEAD_DIM = 128


def shifted(value, axis, by):
    count = lax.axis_size(axis)
    pairs = [(i, i + by) for i in range(count) if 0 <= i + by < count]
    return lax.ppermute(value, axis, pairs)


def shifted_2(value, axis, by):
    count = lax.axis_size(axis)
    return lax.ppermute(value, axis, [(i, (i + by) % count) for i in range(count)])


def block_terms(
    query_rows,
    dout_rows,
    norm_rows,
    delta_rows,
    query_ids,
    query_start,
    key_rows,
    value_rows,
    key_ids,
    key_start,
):
    r = query_rows.shape[0]
    c = key_rows.shape[0]
    kv_local = key_rows.shape[1] // HEAD_DIM
    heads_local = query_rows.shape[1] // HEAD_DIM
    group = heads_local // kv_local
    scaling = HEAD_DIM ** (-0.5)
    query_heads = query_rows.reshape(r, kv_local, group, HEAD_DIM)
    dout_heads = dout_rows.reshape(r, kv_local, group, HEAD_DIM)
    key_heads = key_rows.reshape(c, kv_local, HEAD_DIM)
    value_heads = value_rows.reshape(c, kv_local, HEAD_DIM)
    scores = (
        jnp.einsum("qgjd,kgd->gjqk", query_heads, key_heads, preferred_element_type=jnp.float32)
        * scaling
    )
    norm_cols = jnp.transpose(norm_rows.reshape(r, kv_local, group), (1, 2, 0))[..., None]
    delta_cols = jnp.transpose(delta_rows.reshape(r, kv_local, group), (1, 2, 0))[..., None]
    query_pos = query_start + jnp.arange(r, dtype=jnp.int32)
    key_pos = key_start + jnp.arange(c, dtype=jnp.int32)
    allowed = (query_ids[:, None] == key_ids[None, :]) & (query_pos[:, None] >= key_pos[None, :])
    weights = jnp.where(allowed, jnp.exp(scores - norm_cols), 0.0)
    weights_low = weights.astype(jnp.bfloat16)
    grad_value = jnp.einsum(
        "gjqk,qgjd->kgd", weights_low, dout_heads, preferred_element_type=jnp.float32
    )
    prob_grad = jnp.einsum(
        "qgjd,kgd->gjqk", dout_heads, value_heads, preferred_element_type=jnp.float32
    )
    score_grad = (weights * (prob_grad - delta_cols)).astype(jnp.bfloat16)
    grad_query = (
        jnp.einsum("gjqk,kgd->qgjd", score_grad, key_heads, preferred_element_type=jnp.float32)
        * scaling
    )
    grad_key = (
        jnp.einsum("gjqk,qgjd->kgd", score_grad, query_heads, preferred_element_type=jnp.float32)
        * scaling
    )
    return (
        grad_query.reshape(r, heads_local * HEAD_DIM),
        grad_key.reshape(c, kv_local * HEAD_DIM),
        grad_value.reshape(c, kv_local * HEAD_DIM),
    )


def head_delta(dout_rows, output_rows):
    row_count = dout_rows.shape[0]
    product = dout_rows.astype(jnp.float32) * output_rows.astype(jnp.float32)
    return jnp.sum(product.reshape(row_count, -1, HEAD_DIM), axis=2)


def local(query_in, key_in, value_in, attn_out, out_grad, log_norm, doc_ids):
    query_rows, key_rows, value_rows, dout_rows, output_rows = (
        lax.all_to_all(query_in, "head", split_axis=1, concat_axis=0, tiled=True),
        lax.all_to_all(key_in, "head", split_axis=1, concat_axis=0, tiled=True),
        lax.all_to_all(value_in, "head", split_axis=1, concat_axis=0, tiled=True),
        lax.all_to_all(attn_out, "head", split_axis=1, concat_axis=0, tiled=True),
        lax.all_to_all(out_grad, "head", split_axis=1, concat_axis=0, tiled=True),
    )
    norm_rows = lax.all_to_all(log_norm, "head", split_axis=1, concat_axis=0, tiled=True)
    dout_rows, output_rows = (output_rows, dout_rows)
    delta_rows = head_delta(dout_rows, output_rows)
    row_count = query_rows.shape[0]
    cycle_size = lax.axis_size("ctx")
    my_index = lax.axis_index("ctx")
    my_start = my_index * row_count
    visits = min(cycle_size, row_count // row_count + 1)

    def ids_at(start):
        return lax.dynamic_slice_in_dim(doc_ids, start, row_count)

    my_ids = ids_at(my_start)
    query_zero = jnp.zeros(query_rows.shape, jnp.float32)
    key_zero = jnp.zeros(key_rows.shape, jnp.float32)

    def skipped(_):
        return (query_zero, key_zero, key_zero)

    key_value = jnp.stack((key_rows, value_rows))

    def visit_block(held_pair, grad_pair, source):
        key_start = source * row_count

        def compute(_):
            return block_terms(
                query_rows,
                dout_rows,
                norm_rows,
                delta_rows,
                my_ids,
                my_start,
                held_pair[0],
                held_pair[1],
                ids_at(key_start),
                key_start,
            )

        grad_query, grad_key, grad_value = lax.cond(source <= my_index, compute, skipped, 0)
        return (grad_query, grad_pair + jnp.stack((grad_key, grad_value)))

    def cycle_turn(turn_index, carry):
        held_pair, grad_pair, query_total = carry
        following = shifted(held_pair, "ctx", 1)
        grad_query, grad_pair = visit_block(
            held_pair, grad_pair, (my_index - turn_index) % cycle_size
        )
        grad_pair = shifted_2(grad_pair, "ctx", 1)
        return (following, grad_pair, query_total + grad_query)

    start = (key_value, jnp.zeros(key_value.shape, jnp.float32), query_zero)
    held_pair, grad_pair, query_total = lax.fori_loop(0, visits - 1, cycle_turn, start)
    grad_query, grad_pair = visit_block(
        held_pair, grad_pair, (my_index - (visits - 1)) % cycle_size
    )
    grad_pair = shifted_2(grad_pair.astype(jnp.bfloat16), "ctx", 1 - visits).astype(grad_pair.dtype)
    query_total = query_total + grad_query
    key_total = grad_pair[0]
    value_total = grad_pair[1]
    query_grad, key_grad, value_grad = (
        lax.all_to_all(
            query_total.astype(jnp.bfloat16), "head", split_axis=0, concat_axis=1, tiled=True
        ),
        lax.all_to_all(
            key_total.astype(jnp.bfloat16), "head", split_axis=0, concat_axis=1, tiled=True
        ),
        lax.all_to_all(
            value_total.astype(jnp.bfloat16), "head", split_axis=0, concat_axis=1, tiled=True
        ),
    )
    return (query_grad, key_grad, value_grad)


def solution(mesh):
    in_specs = (
        P(("ctx", "head"), None),
        P(("ctx", "head"), None),
        P(("ctx", "head"), None),
        P(("ctx", "head"), None),
        P(("ctx", "head"), None),
        P(("ctx", "head"), None),
        P(),
    )
    out_specs = (P(("ctx", "head"), None), P(("ctx", "head"), None), P(("ctx", "head"), None))
    return jax.shard_map(local, mesh=mesh, in_specs=in_specs, out_specs=out_specs, check_vma=False)
```

profile of v0, /device:TPU:8, one launch (start us, length us, event | category | flops | bytes accessed | tf_op | source)
XLA Modules:
  0.0 171.9 jit_solution(2658840993720488320)
XLA Ops:
  2.5 3.7 %all-to-all-start = ((bf16[128,4,256]{0,2,1:T(8,128)(2,1)}), bf16[128,4,256]{0,2,1:T(8,128)(2,1)S(1)}, u32[]{:S(2)}, u32[]{:S(2)}) async-start(bf16[128,4,256]{0,2,1:T(8,128)(2,1)} %bitcast.44), calls=%async_computation | async-start | bytes 524288 | tf_op jit(solution)/shard_map/all_to_all | solution.py:84
  8.0 3.6 %all-to-all-done = bf16[128,4,256]{0,2,1:T(8,128)(2,1)S(1)} async-done(((bf16[128,4,256]{0,2,1:T(8,128)(2,1)}), bf16[128,4,256]{0,2,1:T(8,128)(2,1)S(1)}, u32[]{:S(2)}, u32[]{:S(2)}) %all-to-all-start) | async-done | bytes 262176 | tf_op jit(solution)/shard_map/all_to_all | solution.py:84
  11.6 3.4 %all-to-all-start.1 = ((bf16[128,4,256]{0,2,1:T(8,128)(2,1)}), bf16[128,4,256]{0,2,1:T(8,128)(2,1)S(1)}, u32[]{:S(2)}, u32[]{:S(2)}) async-start(bf16[128,4,256]{0,2,1:T(8,128)(2,1)} %bitcast.47), calls=%async_computation.1 | async-start | bytes 524288 | tf_op jit(solution)/shard_map/all_to_all | solution.py:85
  17.3 3.1 %all-to-all-done.1 = bf16[128,4,256]{0,2,1:T(8,128)(2,1)S(1)} async-done(((bf16[128,4,256]{0,2,1:T(8,128)(2,1)}), bf16[128,4,256]{0,2,1:T(8,128)(2,1)S(1)}, u32[]{:S(2)}, u32[]{:S(2)}) %all-to-all-start.1) | async-done | bytes 262176 | tf_op jit(solution)/shard_map/all_to_all | solution.py:85
  21.1 3.5 %all-to-all-start.5 = ((bf16[128,4,1024]{0,2,1:T(8,128)(2,1)}), bf16[128,4,1024]{0,2,1:T(8,128)(2,1)S(1)}, u32[]{:S(2)}, u32[]{:S(2)}) async-start(bf16[128,4,1024]{0,2,1:T(8,128)(2,1)} %bitcast.59), calls=%async_computation.5 | async-start | bytes 2097152 | tf_op jit(solution)/shard_map/all_to_all | solution.py:86
  26.9 9.0 %all-to-all-done.5 = bf16[128,4,1024]{0,2,1:T(8,128)(2,1)S(1)} async-done(((bf16[128,4,1024]{0,2,1:T(8,128)(2,1)}), bf16[128,4,1024]{0,2,1:T(8,128)(2,1)S(1)}, u32[]{:S(2)}, u32[]{:S(2)}) %all-to-all-start.5) | async-done | bytes 1048608 | tf_op jit(solution)/shard_map/all_to_all | solution.py:86
  35.9 3.5 %all-to-all-start.4 = ((bf16[128,4,1024]{0,2,1:T(8,128)(2,1)}), bf16[128,4,1024]{0,2,1:T(8,128)(2,1)S(1)}, u32[]{:S(2)}, u32[]{:S(2)}) async-start(bf16[128,4,1024]{0,2,1:T(8,128)(2,1)} %bitcast.56), calls=%async_computation.4 | async-start | bytes 2097152 | tf_op jit(solution)/shard_map/all_to_all | solution.py:87
  40.7 11.8 %all-to-all-done.4 = bf16[128,4,1024]{0,2,1:T(8,128)(2,1)S(1)} async-done(((bf16[128,4,1024]{0,2,1:T(8,128)(2,1)}), bf16[128,4,1024]{0,2,1:T(8,128)(2,1)S(1)}, u32[]{:S(2)}, u32[]{:S(2)}) %all-to-all-start.4) | async-done | bytes 1048608 | tf_op jit(solution)/shard_map/all_to_all | solution.py:87
  52.5 3.5 %all-to-all-start.2 = ((bf16[128,4,1024]{0,2,1:T(8,128)(2,1)}), bf16[128,4,1024]{0,2,1:T(8,128)(2,1)S(1)}, u32[]{:S(2)}, u32[]{:S(2)}) async-start(bf16[128,4,1024]{0,2,1:T(8,128)(2,1)} %bitcast.177), calls=%async_computation.2 | async-start | bytes 2097152 | tf_op jit(solution)/shard_map/all_to_all | solution.py:83
  62.4 6.7 %all-to-all-done.2 = bf16[128,4,1024]{0,2,1:T(8,128)(2,1)S(1)} async-done(((bf16[128,4,1024]{0,2,1:T(8,128)(2,1)}), bf16[128,4,1024]{0,2,1:T(8,128)(2,1)S(1)}, u32[]{:S(2)}, u32[]{:S(2)}) %all-to-all-start.2) | async-done | bytes 1048608 | tf_op jit(solution)/shard_map/all_to_all | solution.py:83
  69.2 3.3 %all-to-all-start.3 = ((f32[128,4,8]{0,2,1:T(8,128)}), f32[128,4,8]{0,2,1:T(8,128)S(1)}, u32[]{:S(2)}, u32[]{:S(2)}) async-start(f32[128,4,8]{0,2,1:T(8,128)} %bitcast.53), calls=%async_computation.3 | async-start | bytes 32768 | tf_op jit(solution)/shard_map/all_to_all | solution.py:89
  77.1 18.2 %conditional.2 = (f32[512,1024]{0,1:T(8,128)}, f32[1,512,256]{1,2,0:T(8,128)}, f32[1,512,256]{1,2,0:T(8,128)}) conditional(s32[]{:T(128)} %convert_element_type.49, () %tuple.34, (s32[512]{0:T(512)S(1)}, s32[]{:T(128)}, s32[4096]{0:T(1024)}, s32[]{:T(128)}, bf16[2,512,256]{2,1,0:T(8,128)(2,1)}, /*index=5*/bf16[512,1024]{1,0:T(8,128)(2,1)S(1)}, ...), branch_computations={%region_1.2_spmd, %region_2.3_spmd} | conditional | flops 2706768896 | bytes 60457152 | solution.py:127
  85.3 2.7 %fusion.5 = f32[2,512,128,1]{1,2,3,0:T(8,128)} fusion(bf16[512,2,4,128]{0,3,2,1:T(8,128)(2,1)S(1)} %bitcast.184, f32[2,512,512,4]{2,1,3,0:T(8,128)S(1)} %fusion.26, f32[2,4,512]{2,1,0:T(4,128)S(1)} %bitcast.198, pred[512,512]{0,1:T(8,128)(4,1)S(1)} %copy-done.7), kind=kOutput, calls=%fused_computation.7 | convolution fusion | flops 545259520 | bytes 10240000 | tf_op jit(solution)/shard_map/while/body/eval_jaxpr/cond/branch_1_fun/gjqk,qgjd->kgd/dot_general | solution.py:53
  88.0 3.0 %fusion.1 = bf16[2,4,512,512]{2,3,1,0:T(8,128)(2,1)S(1)} fusion(f32[2,512,512,4]{2,1,3,0:T(8,128)S(1)} %fusion.26, f32[2,4,512]{2,1,0:T(4,128)S(1)} %bitcast.196, f32[2,4,512]{2,1,0:T(4,128)S(1)} %bitcast.199, pred[512,512]{0,1:T(8,128)(4,1)S(1)} %copy-done.7, bf16[512,2,128,1]{0,2,3,1:T(8,128)(2,1)S(1)} %bitcast.192, bf16[512,2,4,128]{0,3,2,1:T(8,128)(2,1)S(1)} %bitcast.185), kind=kOutput, calls=%fused_computation.2 | convolution fusion | flops 549453824 | bytes 14188544 | tf_op jit(solution)/shard_map/while/body/eval_jaxpr/cond/branch_1_fun/qgjd,kgd->gjqk/dot_general | solution.py:56
  97.6 3.6 %collective-permute-start = (bf16[2,512,256]{2,1,0:T(8,128)(2,1)}, bf16[2,512,256]{2,1,0:T(8,128)(2,1)S(1)}, u32[]{:S(2)}, u32[]{:S(2)}) collective-permute-start(bf16[2,512,256]{2,1,0:T(8,128)(2,1)} %pad_maximum_fusion.1), channel_id=1, source_target_pairs={{0,1},{1,2},{2,3},{3,4},{4,5},{5,6},{6,7},{8,9},{9,10},{10,11},{11... | collective-permute-start | bytes 1572872 | tf_op jit(solution)/shard_map/while/body/eval_jaxpr/ppermute | solution.py:12
  101.2 16.4 %collective-permute-done = bf16[2,512,256]{2,1,0:T(8,128)(2,1)S(1)} collective-permute-done((bf16[2,512,256]{2,1,0:T(8,128)(2,1)}, bf16[2,512,256]{2,1,0:T(8,128)(2,1)S(1)}, u32[]{:S(2)}, u32[]{:S(2)}) %collective-permute-start) | collective-permute-done | bytes 524320 | tf_op jit(solution)/shard_map/while/body/eval_jaxpr/ppermute | solution.py:12
  117.7 14.9 %conditional.3 = (f32[512,1024]{0,1:T(8,128)}, f32[1,512,256]{1,2,0:T(8,128)}, f32[1,512,256]{1,2,0:T(8,128)S(1)}) conditional(s32[]{:T(128)} %convert_element_type.53, () %tuple.36, (s32[512]{0:T(512)S(1)}, s32[]{:T(128)}, s32[4096]{0:T(1024)}, s32[]{:T(128)}, bf16[2,512,256]{2,1,0:T(8,128)(2,1)S(1)}, /*index=5*/bf16[512,1024]{1,0:T(8,128)(2,1)S(1)}, ...), branch_computations={%region_3.4_spmd, %region_4.5_spmd} | conditional | flops 2706768896 | bytes 59408520 | solution.py:127
  125.2 3.0 %fusion.12 = bf16[2,4,512,512]{2,3,1,0:T(8,128)(2,1)S(1)} fusion(f32[2,512,512,4]{2,1,3,0:T(8,128)S(1)} %fusion.27, f32[2,4,512]{2,1,0:T(4,128)S(1)} %bitcast.197, f32[2,4,512]{2,1,0:T(4,128)S(1)} %bitcast.201, pred[512,512]{0,1:T(8,128)(4,1)S(1)} %compare_and_fusion.1, bf16[512,2,128,1]{0,2,3,1:T(8,128)(2,1)S(1)} %bitcast.193, ...), kind=kOutput, calls=%fused_computation.19 | convolution fusion | flops 549453824 | bytes 14188544 | tf_op jit(solution)/shard_map/cond/branch_1_fun/qgjd,kgd->gjqk/dot_general | solution.py:56
  136.4 3.7 %all-to-all-start.6 = ((bf16[4,128,1024]{2,1,0:T(8,128)(2,1)}), bf16[4,128,1024]{2,1,0:T(8,128)(2,1)S(1)}, u32[]{:S(2)}, u32[]{:S(2)}) async-start(bf16[4,128,1024]{2,1,0:T(8,128)(2,1)} %bitcast.64), calls=%async_computation.6 | async-start | bytes 2097152 | tf_op jit(solution)/shard_map/all_to_all | solution.py:149
  141.8 6.7 %collective-permute-done.2 = bf16[2,512,256]{1,2,0:T(8,128)(2,1)S(1)} collective-permute-done((bf16[2,512,256]{1,2,0:T(8,128)(2,1)S(1)}, bf16[2,512,256]{1,2,0:T(8,128)(2,1)S(1)}, u32[]{:S(2)}, u32[]{:S(2)}) %collective-permute-start.2) | collective-permute-done | bytes 524320 | tf_op jit(solution)/shard_map/ppermute | solution.py:17
  149.3 4.0 %all-to-all-done.6 = bf16[4,128,1024]{2,1,0:T(8,128)(2,1)S(1)} async-done(((bf16[4,128,1024]{2,1,0:T(8,128)(2,1)}), bf16[4,128,1024]{2,1,0:T(8,128)(2,1)S(1)}, u32[]{:S(2)}, u32[]{:S(2)}) %all-to-all-start.6) | async-done | bytes 1048608 | tf_op jit(solution)/shard_map/all_to_all | solution.py:149
  153.3 3.4 %all-to-all-start.8 = ((bf16[4,128,256]{2,1,0:T(8,128)(2,1)}), bf16[4,128,256]{2,1,0:T(8,128)(2,1)S(1)}, u32[]{:S(2)}, u32[]{:S(2)}) async-start(bf16[4,128,256]{2,1,0:T(8,128)(2,1)} %bitcast.70), calls=%async_computation.8 | async-start | bytes 524288 | tf_op jit(solution)/shard_map/all_to_all | solution.py:155
  157.6 4.5 %all-to-all-done.8 = bf16[4,128,256]{2,1,0:T(8,128)(2,1)S(1)} async-done(((bf16[4,128,256]{2,1,0:T(8,128)(2,1)}), bf16[4,128,256]{2,1,0:T(8,128)(2,1)S(1)}, u32[]{:S(2)}, u32[]{:S(2)}) %all-to-all-start.8) | async-done | bytes 262176 | tf_op jit(solution)/shard_map/all_to_all | solution.py:155
  162.1 3.4 %all-to-all-start.7 = ((bf16[4,128,256]{2,1,0:T(8,128)(2,1)}), bf16[4,128,256]{2,1,0:T(8,128)(2,1)S(1)}, u32[]{:S(2)}, u32[]{:S(2)}) async-start(bf16[4,128,256]{2,1,0:T(8,128)(2,1)} %bitcast.67), calls=%async_computation.7 | async-start | bytes 524288 | tf_op jit(solution)/shard_map/all_to_all | solution.py:152
  (78 shorter events, 61.4 us)
Async XLA Ops:
  0.6 38.8 %copy-start.2 = (bf16[128,4096]{1,0:T(8,128)(2,1)S(1)}, bf16[128,4096]{1,0:T(8,128)(2,1)}, u32[]{:S(2)}) copy-start(bf16[128,4096]{1,0:T(8,128)(2,1)} %param.11) | copy-start | bytes 3145732
  2.5 9.1 %all-to-all-start = ((bf16[128,4,256]{0,2,1:T(8,128)(2,1)}), bf16[128,4,256]{0,2,1:T(8,128)(2,1)S(1)}, u32[]{:S(2)}, u32[]{:S(2)}) async-start(bf16[128,4,256]{0,2,1:T(8,128)(2,1)} %bitcast.44), calls=%async_computation | async-start | bytes 524288 | tf_op jit(solution)/shard_map/all_to_all | solution.py:84
  11.6 8.8 %all-to-all-start.1 = ((bf16[128,4,256]{0,2,1:T(8,128)(2,1)}), bf16[128,4,256]{0,2,1:T(8,128)(2,1)S(1)}, u32[]{:S(2)}, u32[]{:S(2)}) async-start(bf16[128,4,256]{0,2,1:T(8,128)(2,1)} %bitcast.47), calls=%async_computation.1 | async-start | bytes 524288 | tf_op jit(solution)/shard_map/all_to_all | solution.py:85
  20.4 0.7 copy-start.5
  21.1 14.8 %all-to-all-start.5 = ((bf16[128,4,1024]{0,2,1:T(8,128)(2,1)}), bf16[128,4,1024]{0,2,1:T(8,128)(2,1)S(1)}, u32[]{:S(2)}, u32[]{:S(2)}) async-start(bf16[128,4,1024]{0,2,1:T(8,128)(2,1)} %bitcast.59), calls=%async_computation.5 | async-start | bytes 2097152 | tf_op jit(solution)/shard_map/all_to_all | solution.py:86
  35.9 16.6 %all-to-all-start.4 = ((bf16[128,4,1024]{0,2,1:T(8,128)(2,1)}), bf16[128,4,1024]{0,2,1:T(8,128)(2,1)S(1)}, u32[]{:S(2)}, u32[]{:S(2)}) async-start(bf16[128,4,1024]{0,2,1:T(8,128)(2,1)} %bitcast.56), calls=%async_computation.4 | async-start | bytes 2097152 | tf_op jit(solution)/shard_map/all_to_all | solution.py:87
  52.5 16.6 %all-to-all-start.2 = ((bf16[128,4,1024]{0,2,1:T(8,128)(2,1)}), bf16[128,4,1024]{0,2,1:T(8,128)(2,1)S(1)}, u32[]{:S(2)}, u32[]{:S(2)}) async-start(bf16[128,4,1024]{0,2,1:T(8,128)(2,1)} %bitcast.177), calls=%async_computation.2 | async-start | bytes 2097152 | tf_op jit(solution)/shard_map/all_to_all | solution.py:83
  69.2 4.9 %copy-start = (bf16[128,4,1024]{0,2,1:T(8,128)(2,1)}, bf16[128,4,1024]{0,2,1:T(8,128)(2,1)S(1)}, u32[]{:S(2)}) copy-start(bf16[128,4,1024]{0,2,1:T(8,128)(2,1)S(1)} %all-to-all-done.2) | copy-start | bytes 3145732
  69.2 7.9 %all-to-all-start.3 = ((f32[128,4,8]{0,2,1:T(8,128)}), f32[128,4,8]{0,2,1:T(8,128)S(1)}, u32[]{:S(2)}, u32[]{:S(2)}) async-start(f32[128,4,8]{0,2,1:T(8,128)} %bitcast.53), calls=%async_computation.3 | async-start | bytes 32768 | tf_op jit(solution)/shard_map/all_to_all | solution.py:89
  82.9 2.4 %copy-start.3 = (bf16[512,1024]{0,1:T(8,128)(2,1)S(1)}, bf16[512,1024]{0,1:T(8,128)(2,1)}, u32[]{:S(2)}) copy-start(bf16[512,1024]{0,1:T(8,128)(2,1)} %copy.139) | copy-start | bytes 3145732 | tf_op jit(solution)/shard_map/while/body/eval_jaxpr/cond
  82.9 2.4 %copy-start.7 = (pred[512,512]{0,1:T(8,128)(4,1)S(1)}, pred[512,512]{0,1:T(8,128)(4,1)}, u32[]{:S(2)}) copy-start(pred[512,512]{0,1:T(8,128)(4,1)} %compare_and_fusion) | copy-start | bytes 786436 | tf_op jit(solution)/shard_map/while/body/eval_jaxpr/cond
  85.3 2.7 %copy-start.8 = (bf16[1,512,256]{1,2,0:T(8,128)(2,1)S(1)}, bf16[1,512,256]{1,2,0:T(8,128)(2,1)}, u32[]{:S(2)}) copy-start(bf16[1,512,256]{1,2,0:T(8,128)(2,1)} %get-tuple-element.158) | copy-start | bytes 786436 | tf_op jit(solution)/shard_map/while/body/eval_jaxpr/cond
  88.0 5.2 %copy-start.1 = (bf16[1,512,256]{1,2,0:T(8,128)(2,1)S(1)}, bf16[1,512,256]{1,2,0:T(8,128)(2,1)}, u32[]{:S(2)}) copy-start(bf16[1,512,256]{1,2,0:T(8,128)(2,1)} %get-tuple-element.159) | copy-start | bytes 786436 | tf_op jit(solution)/shard_map/while/body/eval_jaxpr/cond
  97.6 42.6 %collective-permute-start.1 = (f32[2,512,256]{1,2,0:T(8,128)}, f32[2,512,256]{1,2,0:T(8,128)}, u32[]{:S(2)}, u32[]{:S(2)}) collective-permute-start(f32[2,512,256]{1,2,0:T(8,128)} %pad_maximum_fusion), channel_id=1, source_target_pairs={{0,1},{1,2},{2,3},{3,4},{4,5},{5,6},{6,7},{7,0},{8,9},{9,10},{10,1... | collective-permute-start | bytes 3145736 | tf_op jit(solution)/shard_map/while/body/eval_jaxpr/ppermute | solution.py:17
  97.6 20.0 %collective-permute-start = (bf16[2,512,256]{2,1,0:T(8,128)(2,1)}, bf16[2,512,256]{2,1,0:T(8,128)(2,1)S(1)}, u32[]{:S(2)}, u32[]{:S(2)}) collective-permute-start(bf16[2,512,256]{2,1,0:T(8,128)(2,1)} %pad_maximum_fusion.1), channel_id=1, source_target_pairs={{0,1},{1,2},{2,3},{3,4},{4,5},{5,6},{6,7},{8,9},{9,10},{10,11},{11... | collective-permute-start | bytes 1572872 | tf_op jit(solution)/shard_map/while/body/eval_jaxpr/ppermute | solution.py:12
  117.7 0.9 copy-start.6
  122.0 1.3 copy-start.4
  136.4 16.9 %all-to-all-start.6 = ((bf16[4,128,1024]{2,1,0:T(8,128)(2,1)}), bf16[4,128,1024]{2,1,0:T(8,128)(2,1)S(1)}, u32[]{:S(2)}, u32[]{:S(2)}) async-start(bf16[4,128,1024]{2,1,0:T(8,128)(2,1)} %bitcast.64), calls=%async_computation.6 | async-start | bytes 2097152 | tf_op jit(solution)/shard_map/all_to_all | solution.py:149
  141.7 6.8 %collective-permute-start.2 = (bf16[2,512,256]{1,2,0:T(8,128)(2,1)S(1)}, bf16[2,512,256]{1,2,0:T(8,128)(2,1)S(1)}, u32[]{:S(2)}, u32[]{:S(2)}) collective-permute-start(bf16[2,512,256]{1,2,0:T(8,128)(2,1)S(1)} %fusion.22), channel_id=1, source_target_pairs={{0,7},{1,0},{2,1},{3,2},{4,3},{5,4},{6,5},{7,6},{8,15},{9,8},{10,9... | collective-permute-start | bytes 1572872 | tf_op jit(solution)/shard_map/ppermute | solution.py:17
  153.3 8.8 %all-to-all-start.8 = ((bf16[4,128,256]{2,1,0:T(8,128)(2,1)}), bf16[4,128,256]{2,1,0:T(8,128)(2,1)S(1)}, u32[]{:S(2)}, u32[]{:S(2)}) async-start(bf16[4,128,256]{2,1,0:T(8,128)(2,1)} %bitcast.70), calls=%async_computation.8 | async-start | bytes 524288 | tf_op jit(solution)/shard_map/all_to_all | solution.py:155
  162.1 8.8 %all-to-all-start.7 = ((bf16[4,128,256]{2,1,0:T(8,128)(2,1)}), bf16[4,128,256]{2,1,0:T(8,128)(2,1)S(1)}, u32[]{:S(2)}, u32[]{:S(2)}) async-start(bf16[4,128,256]{2,1,0:T(8,128)(2,1)} %bitcast.67), calls=%async_computation.7 | async-start | bytes 524288 | tf_op jit(solution)/shard_map/all_to_all | solution.py:152
where the time goes:
time: 173 us; the launch traced here: 172 us
  waiting for transfers between devices  68.6 us (40%)
  starting transfers between devices  35.1 us (20%)
  local copies, waits for them, and re-layouts  32.7 us (19%)
  matrix products  22.8 us (13%)
  other arithmetic  11.7 us (7%)
    ppermute x1, waiting for transfers between devices, shifted(): return lax.ppermute(value, axis, pairs)  16.4 us
    unnamed x15, local copies, waits for them, and re-layouts  13.7 us
    all_to_all x1, waiting for transfers between devices, local(): lax.all_to_all(out_grad, 'head', split_axis=1, concat_axis=0, tiled=True)  11.8 us
    all_to_all x1, waiting for transfers between devices, local(): lax.all_to_all(attn_out, 'head', split_axis=1, concat_axis=0, tiled=True)  9.04 us
    all_to_all x1, waiting for transfers between devices, local(): lax.all_to_all(query_in, 'head', split_axis=1, concat_axis=0, tiled=True)  6.73 us
    ppermute x2, waiting for transfers between devices, shifted_2(): lax.ppermute(value, axis, [(i, (i + by) % count) for i in range(count)])  6.69 us
    another operation x8, local copies, waits for them, and re-layouts  6.4 us
    dot_general x2, matrix products, block_terms(): jnp.einsum('qgjd,kgd->gjqk', dout_heads, value_heads, preferred_element_t...  5.95 us
  transfers between devices with their start and end apart: 12, of which 11 were waited for; matrix products, arithmetic and copies ran while one was open for 25% of the time, Pallas kernels for 0%

commit v1 on v0

--- a/solution.py
+++ b/solution.py
@@ -4,6 +4,13 @@
 from jax.sharding import PartitionSpec as P
 
 HEAD_DIM = 128
+
+
+def stops_all_produce(target, join_dim, axis_k):
+    w2 = lax.axis_size("head")
+    step_out = jnp.split(target, w2, join_dim)
+    now = jnp.stack(step_out, 0)
+    return jnp.concatenate(lax.all_to_all(now, "head", 0, 0), axis=axis_k)
 
 
 def shifted(value, axis, by):
@@ -84,7 +91,7 @@
         lax.all_to_all(key_in, "head", split_axis=1, concat_axis=0, tiled=True),
         lax.all_to_all(value_in, "head", split_axis=1, concat_axis=0, tiled=True),
         lax.all_to_all(attn_out, "head", split_axis=1, concat_axis=0, tiled=True),
-        lax.all_to_all(out_grad, "head", split_axis=1, concat_axis=0, tiled=True),
+        stops_all_produce(out_grad, 1, 0),
     )
     norm_rows = lax.all_to_all(log_norm, "head", split_axis=1, concat_axis=0, tiled=True)
     dout_rows, output_rows = (output_rows, dout_rows)

time: 173 us -> 176 us (1.017)
  waiting for transfers between devices: 68.6 us -> 73 us
  local copies, waits for them, and re-layouts: 32.7 us -> 30.8 us
    all_to_all x1, waiting for transfers between devices: 9.04 us -> 11.9 us  [local(): lax.all_to_all(attn_out, 'head', split_axis=1, concat_axis=0, tiled=True)]
    unnamed x15 -> x12, local copies, waits for them, and re-layouts: 13.7 us -> 11 us
    another operation x8 -> x11, local copies, waits for them, and re-layouts: 6.4 us -> 7.78 us  [the longest x4 4.99 us: block_terms(): dout_heads = dout_rows.reshape(r, kv_local, group, HEAD_DIM)]
  transfers between devices with their start and end apart: 12 -> 12, of which waited for: 11 -> 11; matrix products, arithmetic and copies ran while one was open for 25% -> 24% of each run, Pallas kernels for 0% -> 0%
where the time goes in v1:
time: 176 us; the launch traced here: 175 us
  waiting for transfers between devices  73 us (41%)
  starting transfers between devices  35.5 us (20%)
  local copies, waits for them, and re-layouts  30.8 us (18%)
  matrix products  23.5 us (13%)
  other arithmetic  11.4 us (6%)
    ppermute x1, waiting for transfers between devices, shifted(): return lax.ppermute(value, axis, pairs)  16.4 us
    all_to_all x1, waiting for transfers between devices, local(): lax.all_to_all(attn_out, 'head', split_axis=1, concat_axis=0, tiled=True)  11.9 us
    unnamed x12, local copies, waits for them, and re-layouts  11 us
    all_to_all x1, waiting for transfers between devices, stops_all_produce(): return jnp.concatenate(lax.all_to_all(now, 'head', 0, 0), axis=axis_k)  10.3 us
    all_to_all x1, waiting for transfers between devices, local(): lax.all_to_all(query_in, 'head', split_axis=1, concat_axis=0, tiled=True)  8.38 us
    ppermute x2, waiting for transfers between devices, shifted_2(): lax.ppermute(value, axis, [(i, (i + by) % count) for i in range(count)])  6.69 us
    dot_general x2, matrix products, block_terms(): jnp.einsum('qgjd,kgd->gjqk', dout_heads, value_heads, preferred_element_t...  5.92 us
    dot_general x2, matrix products, block_terms(): jnp.einsum('gjqk,qgjd->kgd', weights_low, dout_heads, preferred_element_t...  5.32 us
  transfers between devices with their start and end apart: 12, of which 11 were waited for; matrix products, arithmetic and copies ran while one was open for 24% of the time, Pallas kernels for 0%

profile of v1, /device:TPU:8, one launch (start us, length us, event | category | flops | bytes accessed | tf_op | source)
XLA Modules:
  0.0 175.3 jit_solution(12880726252387524644)
XLA Ops:
  2.5 3.7 %all-to-all-start = ((bf16[128,4,256]{0,2,1:T(8,128)(2,1)}), bf16[128,4,256]{0,2,1:T(8,128)(2,1)S(1)}, u32[]{:S(2)}, u32[]{:S(2)}) async-start(bf16[128,4,256]{0,2,1:T(8,128)(2,1)} %bitcast.42), calls=%async_computation | async-start | bytes 524288 | tf_op jit(solution)/shard_map/all_to_all | solution.py:91
  8.0 3.6 %all-to-all-done = bf16[128,4,256]{0,2,1:T(8,128)(2,1)S(1)} async-done(((bf16[128,4,256]{0,2,1:T(8,128)(2,1)}), bf16[128,4,256]{0,2,1:T(8,128)(2,1)S(1)}, u32[]{:S(2)}, u32[]{:S(2)}) %all-to-all-start) | async-done | bytes 262176 | tf_op jit(solution)/shard_map/all_to_all | solution.py:91
  11.6 4.0 %all-to-all-start.1 = ((bf16[128,4,256]{0,2,1:T(8,128)(2,1)}), bf16[128,4,256]{0,2,1:T(8,128)(2,1)}, u32[]{:S(2)}, u32[]{:S(2)}) async-start(bf16[128,4,256]{0,2,1:T(8,128)(2,1)} %bitcast.45), calls=%async_computation.1 | async-start | bytes 524288 | tf_op jit(solution)/shard_map/all_to_all | solution.py:92
  17.9 3.2 %all-to-all-done.1 = bf16[128,4,256]{0,2,1:T(8,128)(2,1)} async-done(((bf16[128,4,256]{0,2,1:T(8,128)(2,1)}), bf16[128,4,256]{0,2,1:T(8,128)(2,1)}, u32[]{:S(2)}, u32[]{:S(2)}) %all-to-all-start.1) | async-done | bytes 262176 | tf_op jit(solution)/shard_map/all_to_all | solution.py:92
  21.1 3.5 %all-to-all-start.2 = ((bf16[128,4,1024]{0,2,1:T(8,128)(2,1)}), bf16[128,4,1024]{0,2,1:T(8,128)(2,1)S(1)}, u32[]{:S(2)}, u32[]{:S(2)}) async-start(bf16[128,4,1024]{0,2,1:T(8,128)(2,1)} %bitcast.48), calls=%async_computation.2 | async-start | bytes 2097152 | tf_op jit(solution)/shard_map/all_to_all | solution.py:90
  27.6 8.4 %all-to-all-done.2 = bf16[128,4,1024]{0,2,1:T(8,128)(2,1)S(1)} async-done(((bf16[128,4,1024]{0,2,1:T(8,128)(2,1)}), bf16[128,4,1024]{0,2,1:T(8,128)(2,1)S(1)}, u32[]{:S(2)}, u32[]{:S(2)}) %all-to-all-start.2) | async-done | bytes 1048608 | tf_op jit(solution)/shard_map/all_to_all | solution.py:90
  35.9 3.5 %all-to-all-start.5 = ((bf16[128,4,1024]{2,0,1:T(8,128)(2,1)}), bf16[128,4,1024]{2,0,1:T(8,128)(2,1)S(1)}, u32[]{:S(2)}, u32[]{:S(2)}) async-start(bf16[128,4,1024]{2,0,1:T(8,128)(2,1)} %copy.103), calls=%async_computation.5 | async-start | bytes 2097152 | tf_op jit(solution)/shard_map/all_to_all | solution.py:93
  40.7 11.9 %all-to-all-done.5 = bf16[128,4,1024]{2,0,1:T(8,128)(2,1)S(1)} async-done(((bf16[128,4,1024]{2,0,1:T(8,128)(2,1)}), bf16[128,4,1024]{2,0,1:T(8,128)(2,1)S(1)}, u32[]{:S(2)}, u32[]{:S(2)}) %all-to-all-start.5) | async-done | bytes 1048608 | tf_op jit(solution)/shard_map/all_to_all | solution.py:93
  52.6 3.5 %all-to-all-start.4 = ((bf16[4,128,1024]{2,1,0:T(8,128)(2,1)}), bf16[4,128,1024]{2,1,0:T(8,128)(2,1)S(1)}, u32[]{:S(2)}, u32[]{:S(2)}) async-start(bf16[4,128,1024]{2,1,0:T(8,128)(2,1)} %pad_maximum_fusion), calls=%async_computation.4 | async-start | bytes 2097152 | tf_op jit(solution)/shard_map/all_to_all | solution.py:13
  59.0 10.3 %all-to-all-done.4 = bf16[4,128,1024]{2,1,0:T(8,128)(2,1)S(1)} async-done(((bf16[4,128,1024]{2,1,0:T(8,128)(2,1)}), bf16[4,128,1024]{2,1,0:T(8,128)(2,1)S(1)}, u32[]{:S(2)}, u32[]{:S(2)}) %all-to-all-start.4) | async-done | bytes 1048608 | tf_op jit(solution)/shard_map/all_to_all | solution.py:13
  69.2 3.3 %all-to-all-start.3 = ((f32[128,4,8]{0,2,1:T(8,128)}), f32[128,4,8]{0,2,1:T(8,128)S(1)}, u32[]{:S(2)}, u32[]{:S(2)}) async-start(f32[128,4,8]{0,2,1:T(8,128)} %bitcast.51), calls=%async_computation.3 | async-start | bytes 32768 | tf_op jit(solution)/shard_map/all_to_all | solution.py:96
  77.2 19.3 %conditional.2 = (f32[512,1024]{0,1:T(8,128)}, f32[1,512,256]{1,2,0:T(8,128)}, f32[1,512,256]{1,2,0:T(8,128)}) conditional(s32[]{:T(128)} %convert_element_type.49, () %tuple.34, (s32[512]{0:T(512)S(1)}, s32[]{:T(128)}, s32[4096]{0:T(1024)}, s32[]{:T(128)}, bf16[2,512,256]{2,1,0:T(8,128)(2,1)}, /*index=5*/bf16[512,1024]{1,0:T(8,128)(2,1)S(1)}, ...), branch_computations={%region_1.2_spmd, %region_2.3_spmd} | conditional | flops 2706768896 | bytes 62554304 | solution.py:134
  86.5 2.7 %fusion.5 = f32[2,512,128,1]{1,2,3,0:T(8,128)} fusion(bf16[512,2,4,128]{0,3,2,1:T(8,128)(2,1)S(1)} %copy-done.3, f32[2,512,512,4]{2,1,3,0:T(8,128)S(1)} %fusion.26, f32[2,4,512]{2,1,0:T(4,128)S(1)} %bitcast.192, pred[512,512]{0,1:T(8,128)(4,1)S(1)} %copy-done.5), kind=kOutput, calls=%fused_computation.7 | convolution fusion | flops 545259520 | bytes 10240000 | tf_op jit(solution)/shard_map/while/body/eval_jaxpr/cond/branch_1_fun/gjqk,qgjd->kgd/dot_general | solution.py:60
  89.2 3.0 %fusion.1 = bf16[2,4,512,512]{2,3,1,0:T(8,128)(2,1)S(1)} fusion(f32[2,512,512,4]{2,1,3,0:T(8,128)S(1)} %fusion.26, f32[2,4,512]{2,1,0:T(4,128)S(1)} %bitcast.190, f32[2,4,512]{2,1,0:T(4,128)S(1)} %bitcast.193, pred[512,512]{0,1:T(8,128)(4,1)S(1)} %copy-done.5, bf16[512,2,128,1]{0,2,3,1:T(8,128)(2,1)S(1)} %bitcast.186, bf16[512,2,4,128]{0,3,2,1:T(8,128)(2,1)S(1)} %copy-done.3), kind=kOutput, calls=%fused_computation.2 | convolution fusion | flops 549453824 | bytes 14188544 | tf_op jit(solution)/shard_map/while/body/eval_jaxpr/cond/branch_1_fun/qgjd,kgd->gjqk/dot_general | solution.py:63
  98.8 3.6 %collective-permute-start = (bf16[2,512,256]{2,1,0:T(8,128)(2,1)}, bf16[2,512,256]{2,1,0:T(8,128)(2,1)S(1)}, u32[]{:S(2)}, u32[]{:S(2)}) collective-permute-start(bf16[2,512,256]{2,1,0:T(8,128)(2,1)} %pad_maximum_fusion.2), channel_id=1, source_target_pairs={{0,1},{1,2},{2,3},{3,4},{4,5},{5,6},{6,7},{8,9},{9,10},{10,11},{11... | collective-permute-start | bytes 1572872 | tf_op jit(solution)/shard_map/while/body/eval_jaxpr/ppermute | solution.py:19
  102.4 16.4 %collective-permute-done = bf16[2,512,256]{2,1,0:T(8,128)(2,1)S(1)} collective-permute-done((bf16[2,512,256]{2,1,0:T(8,128)(2,1)}, bf16[2,512,256]{2,1,0:T(8,128)(2,1)S(1)}, u32[]{:S(2)}, u32[]{:S(2)}) %collective-permute-start) | collective-permute-done | bytes 524320 | tf_op jit(solution)/shard_map/while/body/eval_jaxpr/ppermute | solution.py:19
  118.8 17.2 %conditional.3 = (f32[512,1024]{0,1:T(8,128)}, f32[1,512,256]{1,2,0:T(8,128)}, f32[1,512,256]{1,2,0:T(8,128)}) conditional(s32[]{:T(128)} %convert_element_type.53, () %tuple.36, (s32[512]{0:T(512)S(1)}, s32[]{:T(128)}, s32[4096]{0:T(1024)}, s32[]{:T(128)}, bf16[2,512,256]{2,1,0:T(8,128)(2,1)S(1)}, /*index=5*/bf16[512,1024]{1,0:T(8,128)(2,1)S(1)}, ...), branch_computations={%region_3.4_spmd, %region_4.5_spmd} | conditional | flops 2706768896 | bytes 61505704 | solution.py:134
  128.7 3.0 %fusion.12 = bf16[2,4,512,512]{2,3,1,0:T(8,128)(2,1)S(1)} fusion(f32[2,512,512,4]{2,1,3,0:T(8,128)S(1)} %fusion.27, f32[2,4,512]{2,1,0:T(4,128)S(1)} %bitcast.191, f32[2,4,512]{2,1,0:T(4,128)S(1)} %bitcast.195, pred[512,512]{0,1:T(8,128)(4,1)S(1)} %copy-done.6, bf16[512,2,128,1]{0,2,3,1:T(8,128)(2,1)S(1)} %bitcast.187, ...), kind=kOutput, calls=%fused_computation.19 | convolution fusion | flops 549453824 | bytes 14188544 | tf_op jit(solution)/shard_map/cond/branch_1_fun/qgjd,kgd->gjqk/dot_general | solution.py:63
  139.9 3.5 %all-to-all-start.6 = ((bf16[4,128,1024]{2,1,0:T(8,128)(2,1)}), bf16[4,128,1024]{2,1,0:T(8,128)(2,1)S(1)}, u32[]{:S(2)}, u32[]{:S(2)}) async-start(bf16[4,128,1024]{2,1,0:T(8,128)(2,1)} %bitcast.62), calls=%async_computation.6 | async-start | bytes 2097152 | tf_op jit(solution)/shard_map/all_to_all | solution.py:156
  145.2 6.7 %collective-permute-done.2 = bf16[2,512,256]{1,2,0:T(8,128)(2,1)S(1)} collective-permute-done((bf16[2,512,256]{1,2,0:T(8,128)(2,1)S(1)}, bf16[2,512,256]{1,2,0:T(8,128)(2,1)S(1)}, u32[]{:S(2)}, u32[]{:S(2)}) %collective-permute-start.2) | collective-permute-done | bytes 524320 | tf_op jit(solution)/shard_map/ppermute | solution.py:24
  152.8 4.0 %all-to-all-done.6 = bf16[4,128,1024]{2,1,0:T(8,128)(2,1)S(1)} async-done(((bf16[4,128,1024]{2,1,0:T(8,128)(2,1)}), bf16[4,128,1024]{2,1,0:T(8,128)(2,1)S(1)}, u32[]{:S(2)}, u32[]{:S(2)}) %all-to-all-start.6) | async-done | bytes 1048608 | tf_op jit(solution)/shard_map/all_to_all | solution.py:156
  156.8 3.4 %all-to-all-start.8 = ((bf16[4,128,256]{2,1,0:T(8,128)(2,1)}), bf16[4,128,256]{2,1,0:T(8,128)(2,1)S(1)}, u32[]{:S(2)}, u32[]{:S(2)}) async-start(bf16[4,128,256]{2,1,0:T(8,128)(2,1)} %bitcast.68), calls=%async_computation.8 | async-start | bytes 524288 | tf_op jit(solution)/shard_map/all_to_all | solution.py:162
  161.1 4.5 %all-to-all-done.8 = bf16[4,128,256]{2,1,0:T(8,128)(2,1)S(1)} async-done(((bf16[4,128,256]{2,1,0:T(8,128)(2,1)}), bf16[4,128,256]{2,1,0:T(8,128)(2,1)S(1)}, u32[]{:S(2)}, u32[]{:S(2)}) %all-to-all-start.8) | async-done | bytes 262176 | tf_op jit(solution)/shard_map/all_to_all | solution.py:162
  165.6 3.4 %all-to-all-start.7 = ((bf16[4,128,256]{2,1,0:T(8,128)(2,1)}), bf16[4,128,256]{2,1,0:T(8,128)(2,1)S(1)}, u32[]{:S(2)}, u32[]{:S(2)}) async-start(bf16[4,128,256]{2,1,0:T(8,128)(2,1)} %bitcast.65), calls=%async_computation.7 | async-start | bytes 524288 | tf_op jit(solution)/shard_map/all_to_all | solution.py:159
  (80 shorter events, 61.3 us)
Async XLA Ops:
  0.6 38.8 %copy-start.2 = (bf16[128,4096]{1,0:T(8,128)(2,1)S(1)}, bf16[128,4096]{1,0:T(8,128)(2,1)}, u32[]{:S(2)}) copy-start(bf16[128,4096]{1,0:T(8,128)(2,1)} %param.15) | copy-start | bytes 3145732
  2.5 9.1 %all-to-all-start = ((bf16[128,4,256]{0,2,1:T(8,128)(2,1)}), bf16[128,4,256]{0,2,1:T(8,128)(2,1)S(1)}, u32[]{:S(2)}, u32[]{:S(2)}) async-start(bf16[128,4,256]{0,2,1:T(8,128)(2,1)} %bitcast.42), calls=%async_computation | async-start | bytes 524288 | tf_op jit(solution)/shard_map/all_to_all | solution.py:91
  11.6 9.5 %all-to-all-start.1 = ((bf16[128,4,256]{0,2,1:T(8,128)(2,1)}), bf16[128,4,256]{0,2,1:T(8,128)(2,1)}, u32[]{:S(2)}, u32[]{:S(2)}) async-start(bf16[128,4,256]{0,2,1:T(8,128)(2,1)} %bitcast.45), calls=%async_computation.1 | async-start | bytes 524288 | tf_op jit(solution)/shard_map/all_to_all | solution.py:92
  21.1 14.8 %all-to-all-start.2 = ((bf16[128,4,1024]{0,2,1:T(8,128)(2,1)}), bf16[128,4,1024]{0,2,1:T(8,128)(2,1)S(1)}, u32[]{:S(2)}, u32[]{:S(2)}) async-start(bf16[128,4,1024]{0,2,1:T(8,128)(2,1)} %bitcast.48), calls=%async_computation.2 | async-start | bytes 2097152 | tf_op jit(solution)/shard_map/all_to_all | solution.py:90
  35.9 16.6 %copy-start = (bf16[128,4,1024]{0,2,1:T(8,128)(2,1)}, bf16[128,4,1024]{0,2,1:T(8,128)(2,1)S(1)}, u32[]{:S(2)}) copy-start(bf16[128,4,1024]{0,2,1:T(8,128)(2,1)S(1)} %all-to-all-done.2) | copy-start | bytes 3145732
  35.9 16.6 %all-to-all-start.5 = ((bf16[128,4,1024]{2,0,1:T(8,128)(2,1)}), bf16[128,4,1024]{2,0,1:T(8,128)(2,1)S(1)}, u32[]{:S(2)}, u32[]{:S(2)}) async-start(bf16[128,4,1024]{2,0,1:T(8,128)(2,1)} %copy.103), calls=%async_computation.5 | async-start | bytes 2097152 | tf_op jit(solution)/shard_map/all_to_all | solution.py:93
  52.6 16.6 %all-to-all-start.4 = ((bf16[4,128,1024]{2,1,0:T(8,128)(2,1)}), bf16[4,128,1024]{2,1,0:T(8,128)(2,1)S(1)}, u32[]{:S(2)}, u32[]{:S(2)}) async-start(bf16[4,128,1024]{2,1,0:T(8,128)(2,1)} %pad_maximum_fusion), calls=%async_computation.4 | async-start | bytes 2097152 | tf_op jit(solution)/shard_map/all_to_all | solution.py:13
  69.2 7.9 %all-to-all-start.3 = ((f32[128,4,8]{0,2,1:T(8,128)}), f32[128,4,8]{0,2,1:T(8,128)S(1)}, u32[]{:S(2)}, u32[]{:S(2)}) async-start(f32[128,4,8]{0,2,1:T(8,128)} %bitcast.51), calls=%async_computation.3 | async-start | bytes 32768 | tf_op jit(solution)/shard_map/all_to_all | solution.py:96
  84.1 2.4 %copy-start.3 = (bf16[512,2,4,128]{0,3,2,1:T(8,128)(2,1)S(1)}, bf16[512,2,4,128]{0,3,2,1:T(8,128)(2,1)}, u32[]{:S(2)}) copy-start(bf16[512,2,4,128]{0,3,2,1:T(8,128)(2,1)} %copy.124) | copy-start | bytes 3145732 | tf_op jit(solution)/shard_map/while/body/eval_jaxpr/cond
  84.1 2.4 %copy-start.5 = (pred[512,512]{0,1:T(8,128)(4,1)S(1)}, pred[512,512]{0,1:T(8,128)(4,1)}, u32[]{:S(2)}) copy-start(pred[512,512]{0,1:T(8,128)(4,1)} %compare_and_fusion) | copy-start | bytes 786436 | tf_op jit(solution)/shard_map/while/body/eval_jaxpr/cond
  86.5 2.7 %copy-start.7 = (bf16[1,512,256]{1,2,0:T(8,128)(2,1)S(1)}, bf16[1,512,256]{1,2,0:T(8,128)(2,1)}, u32[]{:S(2)}) copy-start(bf16[1,512,256]{1,2,0:T(8,128)(2,1)} %get-tuple-element.173) | copy-start | bytes 786436 | tf_op jit(solution)/shard_map/while/body/eval_jaxpr/cond
  89.2 5.2 %copy-start.1 = (bf16[1,512,256]{1,2,0:T(8,128)(2,1)S(1)}, bf16[1,512,256]{1,2,0:T(8,128)(2,1)}, u32[]{:S(2)}) copy-start(bf16[1,512,256]{1,2,0:T(8,128)(2,1)} %get-tuple-element.174) | copy-start | bytes 786436 | tf_op jit(solution)/shard_map/while/body/eval_jaxpr/cond
  98.8 44.6 %collective-permute-start.1 = (f32[2,512,256]{1,2,0:T(8,128)}, f32[2,512,256]{1,2,0:T(8,128)}, u32[]{:S(2)}, u32[]{:S(2)}) collective-permute-start(f32[2,512,256]{1,2,0:T(8,128)} %pad_maximum_fusion.1), channel_id=1, source_target_pairs={{0,1},{1,2},{2,3},{3,4},{4,5},{5,6},{6,7},{7,0},{8,9},{9,10},{10,1... | collective-permute-start | bytes 3145736 | tf_op jit(solution)/shard_map/while/body/eval_jaxpr/ppermute | solution.py:24
  98.8 20.0 %collective-permute-start = (bf16[2,512,256]{2,1,0:T(8,128)(2,1)}, bf16[2,512,256]{2,1,0:T(8,128)(2,1)S(1)}, u32[]{:S(2)}, u32[]{:S(2)}) collective-permute-start(bf16[2,512,256]{2,1,0:T(8,128)(2,1)} %pad_maximum_fusion.2), channel_id=1, source_target_pairs={{0,1},{1,2},{2,3},{3,4},{4,5},{5,6},{6,7},{8,9},{9,10},{10,11},{11... | collective-permute-start | bytes 1572872 | tf_op jit(solution)/shard_map/while/body/eval_jaxpr/ppermute | solution.py:19
  124.2 1.9 %copy-start.4 = (bf16[512,2,4,128]{0,3,2,1:T(8,128)(2,1)S(1)}, bf16[512,2,4,128]{0,3,2,1:T(8,128)(2,1)}, u32[]{:S(2)}) copy-start(bf16[512,2,4,128]{0,3,2,1:T(8,128)(2,1)} %copy.134) | copy-start | bytes 3145732 | tf_op jit(solution)/shard_map/cond
  124.7 1.3 copy-start.6
  126.0 2.7 %copy-start.8 = (bf16[1,512,256]{1,2,0:T(8,128)(2,1)S(1)}, bf16[1,512,256]{1,2,0:T(8,128)(2,1)}, u32[]{:S(2)}) copy-start(bf16[1,512,256]{1,2,0:T(8,128)(2,1)} %get-tuple-element.177) | copy-start | bytes 786436 | tf_op jit(solution)/shard_map/cond
  139.9 16.9 %all-to-all-start.6 = ((bf16[4,128,1024]{2,1,0:T(8,128)(2,1)}), bf16[4,128,1024]{2,1,0:T(8,128)(2,1)S(1)}, u32[]{:S(2)}, u32[]{:S(2)}) async-start(bf16[4,128,1024]{2,1,0:T(8,128)(2,1)} %bitcast.62), calls=%async_computation.6 | async-start | bytes 2097152 | tf_op jit(solution)/shard_map/all_to_all | solution.py:156
  145.1 6.8 %collective-permute-start.2 = (bf16[2,512,256]{1,2,0:T(8,128)(2,1)S(1)}, bf16[2,512,256]{1,2,0:T(8,128)(2,1)S(1)}, u32[]{:S(2)}, u32[]{:S(2)}) collective-permute-start(bf16[2,512,256]{1,2,0:T(8,128)(2,1)S(1)} %fusion.22), channel_id=1, source_target_pairs={{0,7},{1,0},{2,1},{3,2},{4,3},{5,4},{6,5},{7,6},{8,15},{9,8},{10,9... | collective-permute-start | bytes 1572872 | tf_op jit(solution)/shard_map/ppermute | solution.py:24
  156.8 8.8 %all-to-all-start.8 = ((bf16[4,128,256]{2,1,0:T(8,128)(2,1)}), bf16[4,128,256]{2,1,0:T(8,128)(2,1)S(1)}, u32[]{:S(2)}, u32[]{:S(2)}) async-start(bf16[4,128,256]{2,1,0:T(8,128)(2,1)} %bitcast.68), calls=%async_computation.8 | async-start | bytes 524288 | tf_op jit(solution)/shard_map/all_to_all | solution.py:162
  165.6 8.8 %all-to-all-start.7 = ((bf16[4,128,256]{2,1,0:T(8,128)(2,1)}), bf16[4,128,256]{2,1,0:T(8,128)(2,1)S(1)}, u32[]{:S(2)}, u32[]{:S(2)}) async-start(bf16[4,128,256]{2,1,0:T(8,128)(2,1)} %bitcast.65), calls=%async_computation.7 | async-start | bytes 524288 | tf_op jit(solution)/shard_map/all_to_all | solution.py:159
